TPU v7x, 32 devices: a whole 2x2x4 slice. The times are simulated.
32 devices in a mesh: seq: 16 (over z, y, x), col: 2 (over core).
Axes of the slice: x: 2, y: 2, z: 4, core: 2. Of those that a mesh axis runs over, the one named last changes fastest.
Arguments:
- hidden: bfloat16 [4, 96, 2304], P(None, None, 'seq'), may hold values from -6 to 6
- key_cache: bfloat16 [1152, 128, 2048], P('seq', None, 'col'), may hold values from -300 to 300
- value_cache: bfloat16 [1152, 128, 2048], P('seq', None, 'col'), may hold values from -6 to 6
- page_table: int32 [96, 128], replicated, may hold values from 0 to 1151, as said below
- cache_len: int32 [96], replicated, may hold values from 1 to 16380, as said below
- order: int32 [96], replicated, may hold values from 0 to 95, each once
- route_ids: int32 [4, 96, 2], replicated, may hold values from 0 to 7, all different within a row; in each aligned block of 96 rows (0 to 95, 96 to 191, ..., all dimensions but the last counted through in order) at most 48 rows name the same one
- w_qkv: bfloat16 [2304, 3, 2048], P('seq', None, 'col'), may hold values from -0.125 to 0.125
- w_out: bfloat16 [2048, 2304], P('col', 'seq'), may hold values from -0.125 to 0.125
- w_router: bfloat16 [2304, 8], replicated, may hold values from -0.125 to 0.125
- w_gate_up: bfloat16 [8, 2304, 2, 5760], P('col', None, None, 'seq'), may hold values from -0.125 to 0.125
- w_down: bfloat16 [8, 5760, 2304], P('col', 'seq'), may hold values from -0.109375 to 0.109375
Outputs:
- layer_out: bfloat16 [4, 96, 2304], P(None, None, 'seq')
- new_keys: bfloat16 [4, 96, 2048], P(None, None, 'col')
- new_values: bfloat16 [4, 96, 2048], P(None, None, 'col')
Inputs may be any that keep to these rules, and one draw needn't show every extreme that they name: `cache_len`: one request's cache holds exactly 16380 tokens; 4 requests hold more than 640 tokens, the others at most 640. `page_table`: for request r the entries 0 to ceil((cache_len[r] + 4) / 128) - 1 name pages that no other such entry names; later entries are never read. `order`: each request sits in exactly one batch slot. `route_ids`: the two experts of a row differ; in each step no expert is named by more than 48 requests.
All inputs are finite; a program needn't handle non-finite values.
Results may differ from a plain program's by a relative error of at most 0.011.
Values may be sent and summed in bfloat16 or wider, within the bound.
A program may use at most 256 MiB of HBM per device.

v0:
```python
import jax
import jax.numpy as jnp
from jax import lax
from jax.sharding import PartitionSpec as P

HEAD_DIM = 64
EPSILON = 1e-05
LOWEST = -1e30


def rotate(row_data, positions, head_dim):
    head_count = row_data.shape[1] // head_dim
    half_dim = head_dim // 2
    frequency = jnp.exp(
        -jnp.log(10000.0) * 2.0 * jnp.arange(half_dim, dtype=jnp.float32) / head_dim
    )
    angles = positions.astype(jnp.float32)[:, None] * frequency[None, :]
    cosine = jnp.cos(angles)[:, None, :]
    sines = jnp.sin(angles)[:, None, :]
    by_head = row_data.reshape(row_data.shape[0], head_count, head_dim)
    front_half = by_head[:, :, :half_dim]
    back_half = by_head[:, :, half_dim:]
    turned = jnp.concatenate(
        [front_half * cosine - back_half * sines, back_half * cosine + front_half * sines], axis=2
    )
    return turned.reshape(row_data.shape)


def local(
    hidden,
    key_cache,
    value_cache,
    page_table,
    cache_len,
    order,
    route_ids,
    w_qkv,
    w_out,
    w_router,
    w_gate_up,
    w_down,
):
    step_count = hidden.shape[0]
    requests = hidden.shape[1]
    width_loc = hidden.shape[2]
    pages_loc = key_cache.shape[0]
    page_size = key_cache.shape[1]
    cols_loc = key_cache.shape[2]
    heads_loc = cols_loc // HEAD_DIM
    width_all = width_loc * lax.axis_size("seq")
    experts_loc = w_gate_up.shape[0]
    ff_loc = w_gate_up.shape[3]
    expert_count = w_router.shape[1]
    expert_base = lax.axis_index("col") * experts_loc
    seq_index = lax.axis_index("seq")
    score_scale = HEAD_DIM ** (-0.5)
    placing = (order[:, None] == jnp.arange(requests)[None, :]).astype(jnp.bfloat16)
    needed = (cache_len + step_count + page_size - 1) // page_size
    columns = jnp.arange(page_table.shape[1])
    in_use = columns[None, :] < needed[:, None]
    local_pages = page_table - seq_index * pages_loc
    page_hits = in_use[:, :, None] & (
        local_pages[:, :, None] == jnp.arange(pages_loc)[None, None, :]
    )
    owned_by = jnp.any(page_hits, axis=1)
    page_starts = jnp.sum(jnp.where(page_hits, columns[None, :, None] * page_size, 0), axis=(0, 1))
    page_len = jnp.sum(jnp.where(owned_by, cache_len[:, None], 0), axis=0)
    is_valid = page_starts[:, None] + jnp.arange(page_size)[None, :] < page_len[:, None]
    owner_pages = owned_by.T
    owner_float = owner_pages.astype(jnp.float32)
    owner_half = owner_pages.astype(jnp.bfloat16)
    keys_local = key_cache.reshape(pages_loc, page_size, heads_loc, HEAD_DIM)
    values_local = value_cache.reshape(pages_loc, page_size, heads_loc, HEAD_DIM)
    w_proj = w_qkv.reshape(width_loc, 3 * cols_loc)
    w_pair = w_gate_up.reshape(experts_loc, width_all, 2 * ff_loc)
    expert_ids = jnp.arange(expert_count)
    known_keys = jnp.zeros((step_count, requests, cols_loc), jnp.bfloat16)
    known_values = jnp.zeros((step_count, requests, cols_loc), jnp.bfloat16)
    attend_known_keys = known_keys
    attend_known_values = known_values
    row_count = step_count * requests
    inputs = jnp.einsum("nsc,sr->nrc", hidden, placing, preferred_element_type=jnp.float32).astype(
        jnp.bfloat16
    )
    wide_in = inputs.astype(jnp.float32)
    squares = jnp.sum(wide_in * wide_in, axis=2)
    partial_value = jnp.dot(
        inputs.reshape(row_count, width_loc), w_proj, preferred_element_type=jnp.float32
    )
    squares, partial_value = lax.psum((squares, partial_value), "seq")
    inv_one = lax.rsqrt(squares.reshape(row_count) / width_all + EPSILON)
    partial_value = partial_value * inv_one[:, None]
    positions = (cache_len[None, :] + 0 + jnp.arange(step_count)[:, None]).reshape(row_count)
    query = rotate(partial_value[:, :cols_loc], positions, HEAD_DIM).astype(jnp.bfloat16)
    fresh_key = rotate(partial_value[:, cols_loc : 2 * cols_loc], positions, HEAD_DIM).astype(
        jnp.bfloat16
    )
    fresh_value = partial_value[:, 2 * cols_loc :].astype(jnp.bfloat16)
    attend_known_keys = attend_known_keys.at[0 : 0 + step_count].set(
        fresh_key.reshape(step_count, requests, cols_loc)
    )
    attend_known_values = attend_known_values.at[0 : 0 + step_count].set(
        fresh_value.reshape(step_count, requests, cols_loc)
    )
    query_heads = query.reshape(step_count, requests, heads_loc, HEAD_DIM)
    page_query = jnp.einsum(
        "pr,nrhd->nphd", owner_half, query_heads, preferred_element_type=jnp.float32
    ).astype(jnp.bfloat16)
    scores = (
        jnp.einsum("pthd,nphd->npth", keys_local, page_query, preferred_element_type=jnp.float32)
        * score_scale
    )
    in_page = is_valid[None, :, :, None]
    scores = jnp.where(in_page, scores, LOWEST)
    page_peak = jnp.max(scores, axis=2)
    owner_mask = owner_pages[None, :, :, None]
    req_peak = jnp.max(jnp.where(owner_mask, page_peak[:, :, None, :], LOWEST), axis=1)
    back_peak = jnp.max(jnp.where(owner_mask, req_peak[:, None, :, :], LOWEST), axis=2)
    weights = jnp.where(in_page, jnp.exp(scores - back_peak[:, :, None, :]), 0.0)
    page_total = jnp.sum(weights, axis=2)
    page_sums = jnp.einsum(
        "npth,pthd->nphd",
        weights.astype(jnp.bfloat16),
        values_local,
        preferred_element_type=jnp.float32,
    )
    weight_sum = jnp.einsum("pr,nph->nrh", owner_float, page_total, precision=lax.Precision.HIGHEST)
    value_sum = jnp.einsum(
        "pr,nphd->nrhd", owner_float, page_sums, precision=lax.Precision.HIGHEST
    ).reshape(step_count, requests, cols_loc)
    top_score = lax.pmax(req_peak, "seq")
    rescale = jnp.exp(req_peak - top_score)
    scaled_values = (
        value_sum.reshape(step_count, requests, heads_loc, HEAD_DIM) * rescale[..., None]
    ).reshape(step_count, requests, cols_loc)
    weight_sum, value_sum = lax.psum((weight_sum * rescale, scaled_values), "seq")
    known_heads = attend_known_keys.reshape(step_count, requests, heads_loc, HEAD_DIM)
    fresh_scores = (
        jnp.einsum("nrhd,urhd->nruh", query_heads, known_heads, preferred_element_type=jnp.float32)
        * score_scale
    )
    visible = jnp.arange(step_count)[None, :] <= 0 + jnp.arange(step_count)[:, None]
    seen = visible[:, None, :, None]
    fresh_scores = jnp.where(seen, fresh_scores, LOWEST)
    best_score = jnp.maximum(top_score, jnp.max(fresh_scores, axis=2))
    fresh_weights = jnp.where(seen, jnp.exp(fresh_scores - best_score[:, :, None, :]), 0.0)
    cache_factor = jnp.exp(top_score - best_score)
    denominator = weight_sum * cache_factor + jnp.sum(fresh_weights, axis=2)
    fresh_sums = jnp.einsum(
        "nruh,urhd->nrhd",
        fresh_weights.astype(jnp.bfloat16),
        attend_known_values.reshape(step_count, requests, heads_loc, HEAD_DIM),
        preferred_element_type=jnp.float32,
    )
    numerator = (
        value_sum.reshape(step_count, requests, heads_loc, HEAD_DIM) * cache_factor[..., None]
        + fresh_sums
    )
    attended = (
        (numerator / denominator[..., None]).reshape(row_count, cols_loc).astype(jnp.bfloat16)
    )
    projected = lax.psum(jnp.dot(attended, w_out, preferred_element_type=jnp.float32), "col")
    residual = (wide_in.reshape(row_count, width_loc) + projected).astype(jnp.bfloat16)
    chosen = route_ids.reshape(row_count, 2)
    mid_steps = residual.reshape(step_count, requests, width_loc)
    shard_rows = lax.all_gather(mid_steps, "seq", axis=2, tiled=True)
    flat_rows = shard_rows.reshape(row_count, shard_rows.shape[2])
    pair_sum = jnp.einsum("rc,ecf->ref", flat_rows, w_pair, preferred_element_type=jnp.float32)
    wide_rows = flat_rows.astype(jnp.float32)
    square_sum = jnp.sum(wide_rows * wide_rows, axis=1)
    router_sum = jnp.dot(flat_rows, w_router, preferred_element_type=jnp.float32)
    pair_sum, square_sum, router_sum = (pair_sum, square_sum, router_sum)
    inv_two = lax.rsqrt(square_sum / width_all + EPSILON)
    logits = router_sum * inv_two[:, None]
    first_pick = chosen[:, 0:1] == expert_ids[None, :]
    second_pick = chosen[:, 1:2] == expert_ids[None, :]
    first_share = jax.nn.sigmoid(
        jnp.sum(jnp.where(first_pick, logits, 0.0), axis=1)
        - jnp.sum(jnp.where(second_pick, logits, 0.0), axis=1)
    )
    gate_rows = jnp.where(first_pick, first_share[:, None], 0.0) + jnp.where(
        second_pick, 1.0 - first_share[:, None], 0.0
    )
    gate_local = lax.dynamic_slice_in_dim(gate_rows, expert_base, experts_loc, 1)
    pair_sum = pair_sum * inv_two[:, None, None]
    active = (jax.nn.silu(pair_sum[..., :ff_loc]) * pair_sum[..., ff_loc:]).astype(jnp.bfloat16)
    outputs = jnp.einsum("ref,efd->red", active, w_down, preferred_element_type=jnp.float32)
    weighted = jnp.sum(outputs * gate_local[:, :, None], axis=1)
    spread = lax.psum_scatter(weighted, "seq", scatter_dimension=1, tiled=True)
    mixture = lax.psum(spread, "col")
    layer_rows = (
        (residual.astype(jnp.float32) + mixture)
        .astype(jnp.bfloat16)
        .reshape(step_count, requests, width_loc)
    )
    return (layer_rows, attend_known_keys, attend_known_values)


def solution(mesh):
    placed = (
        P(None, None, "seq"),
        P("seq", None, "col"),
        P("seq", None, "col"),
        P(),
        P(),
        P(),
        P(),
        P("seq", None, "col"),
        P("col", "seq"),
        P(),
        P("col", None, None, "seq"),
        P("col", "seq", None),
    )
    return jax.shard_map(
        local,
        mesh=mesh,
        in_specs=placed,
        out_specs=(P(None, None, "seq"), P(None, None, "col"), P(None, None, "col")),
        check_vma=False,
    )
```

profile of v0, /device:TPU:0, one launch (start us, length us, event | category | flops | bytes accessed | tf_op | source)
XLA Modules:
  0.0 747.3 jit_solution(15203284363969013890)
XLA Ops:
  7.2 1.2 fusion.25
  9.4 1.2 copy.147
  10.6 3.0 fusion.35
  14.5 1.7 fusion.2
  16.3 45.7 %psum.43 = f32[4,96]{1,0:T(4,128)S(1)} all-reduce(f32[4,96]{1,0:T(4,128)S(1)} %get-tuple-element.66), channel_id=1, replica_groups=mesh['seq'=16,'col'=2] {'seq'}, use_global_device_ids=true, to_apply=%region_5.6 | all-reduce | flops 384 | bytes 3072 | tf_op jit(solution)/shard_map/psum | solution.py:90
  62.1 24.6 %copy.109 = bf16[72,128,1024]{1,2,0:T(8,128)(2,1)} copy(bf16[72,128,1024]{2,1,0:T(8,128)(2,1)} %param.21) | data formatting | bytes 37748736 | tf_op args[1]
  86.7 24.7 %copy.114 = bf16[72,128,1024]{1,2,0:T(8,128)(2,1)} copy(bf16[72,128,1024]{2,1,0:T(8,128)(2,1)} %param.22) | data formatting | bytes 37748736 | tf_op args[2]
  111.5 1.1 select_reduce_fusion
  113.7 83.1 %all-reduce.5.cloned.1.call-done = f32[384,3072]{1,0:T(8,128)} async-done(((f32[384,3072]{1,0:T(8,128)}), f32[384,3072]{1,0:T(8,128)}) %all-reduce.5.cloned.1.call-update) | async-done | bytes 4718608 | tf_op jit(solution)/shard_map/psum | solution.py:90
  196.7 2.8 broadcast_multiply_fusion
  199.5 1.6 fusion.34
  204.8 2.6 copy.119
  207.4 2.2 copy.110
  209.6 9.4 %bitcast_reduce_fusion = (f32[4,72,16]{0,2,1:T(8,128)S(1)}, f32[72,16,4,128]{3,2,1,0:T(4,128)S(1)}) fusion(pred[72,128]{1,0:T(8,128)(4,1)S(1)} %add_compare_fusion, bf16[4,72,16,64]{3,0,2,1:T(4,128)(2,1)} %copy.110, bf16[72,128,16,64]{1,3,2,0:T(8,128)(2,1)} %bitcast.105), kind=kOutput, calls=%fused_computation.8 | convolution fusion | flops 77262336 | bytes 21851136 | tf_op jit(solution)/shard_map/pthd,nphd->npth/dot_general | solution.py:110
  220.4 75.9 %pmax.7 = f32[4,96,16]{1,2,0:T(8,128)} all-reduce(f32[4,96,16]{1,2,0:T(8,128)S(1)} %select_reduce_fusion.2), channel_id=1, replica_groups=mesh['seq'=16,'col'=2] {'seq'}, use_global_device_ids=true, to_apply=%region_9.10 | all-reduce | flops 6144 | bytes 49152 | tf_op jit(solution)/shard_map/pmax | solution.py:131
  296.3 1.4 select_reduce_fusion.1
  297.6 3.0 copy.117
  300.7 1.6 multiply_subtract_fusion
  302.4 1.6 convert_element_type.87
  304.0 4.3 copy.118
  308.3 5.3 fusion.36
  313.6 3.7 copy.120
  317.3 1.4 copy.113
  318.7 1.1 fusion.22
  320.5 14.0 %convolution_bitcast_fusion = f32[4,72,16,64]{3,0,2,1:T(4,128)S(1)} fusion(bf16[72,128,16,64]{1,3,2,0:T(8,128)(2,1)} %bitcast.106, f32[72,16,4,128]{3,2,1,0:T(4,128)S(1)} %get-tuple-element.81, f32[4,72,16]{0,2,1:T(8,128)S(1)} %copy.113, pred[72,128]{1,0:T(8,128)(4,1)} %copy-done.12), kind=kOutput, calls=%fused_computation.24 | convolution fusion | flops 78446592 | bytes 22440960 | tf_op jit(solution)/shard_map/npth,pthd->nphd/dot_general | solution.py:121
  334.4 4.2 bitcast_multiply_fusion.1
  338.7 1.6 slice.111
  340.3 1.9 reshape.362
  342.2 5.0 fusion.20
  347.2 1.9 copy.127
  349.1 1.6 fusion.23
  350.7 3.2 copy.125
  353.9 3.7 fusion.12
  357.6 3.1 copy.126
  361.7 72.0 %psum.45 = f32[4,96,16]{1,2,0:T(8,128)S(1)} all-reduce(f32[4,96,16]{1,2,0:T(8,128)S(1)} %fusion.16), channel_id=1, replica_groups=mesh['seq'=16,'col'=2] {'seq'}, use_global_device_ids=true, to_apply=%region_13.14 | all-reduce | flops 6144 | bytes 49152 | tf_op jit(solution)/shard_map/psum | solution.py:136
  434.4 26.6 %all-reduce.7.cloned.1.call-done = f32[4,96,16,64]{1,3,2,0:T(8,128)} async-done(((f32[4,96,16,64]{1,3,2,0:T(8,128)}), f32[4,96,16,64]{1,3,2,0:T(8,128)}) %all-reduce.7.cloned.1.call-update) | async-done | bytes 1572880 | tf_op jit(solution)/shard_map/psum | solution.py:136
  461.1 2.8 fusion.9
  466.8 17.3 %all-reduce.9.cloned.1.call-done = f32[384,144]{0,1:T(8,128)} async-done(((f32[384,144]{0,1:T(8,128)}), f32[384,144]{0,1:T(8,128)}) %all-reduce.9.cloned.1.call-update) | async-done | bytes 221200 | tf_op jit(solution)/shard_map/psum | solution.py:162
  486.2 64.8 %all-gather.2.cloned.1.call-done = bf16[4,96,2304]{1,0,2:T(4,128)(2,1)} async-done(((bf16[4,96,144]{1,0,2:T(4,128)(2,1)}), bf16[4,96,2304]{1,0,2:T(4,128)(2,1)}) %all-gather.2.cloned.1.call-update) | async-done | bytes 1769488 | tf_op jit(solution)/shard_map/all_gather | solution.py:166
  550.9 4.2 multiply_reduce_fusion
  555.3 3.8 copy.132
  559.1 2.1 select_reduce_fusion.4
  561.2 10.3 %broadcast_multiply_fusion.1 = f32[384,4,720]{0,2,1:T(8,128)S(1)} fusion(f32[384]{0:T(512)S(1)} %rsqrt.27, bf16[384,2304,1]{1,0,2:T(8,128)(2,1)} %bitcast.108, bf16[4,2304,720]{1,2,0:T(8,128)(2,1)} %bitcast.117), kind=kOutput, calls=%fused_computation.19 | convolution fusion | flops 5097185280 | bytes 19465728 | tf_op jit(solution)/shard_map/rc,ecf->ref/dot_general | solution.py:168
  571.5 9.8 %fusion = f32[384,2304]{1,0:T(8,128)} fusion(bf16[4,360,2304]{2,1,0:T(8,128)(2,1)} %param.31, f32[384,4]{0,1:T(4,128)S(1)} %select_add_fusion, f32[384,4,720]{0,2,1:T(8,128)S(1)} %broadcast_multiply_fusion.1), kind=kOutput, calls=%fused_computation.1 | convolution fusion | flops 2557550592 | bytes 14604288 | tf_op jit(solution)/shard_map/ref,efd->red/dot_general | solution.py:187
  581.2 5.2 copy.134
  586.5 132.4 %reduce-scatter.2.cloned.1.call-done = f32[384,144]{0,1:T(8,128)} async-done(((f32[384,2304]{0,1:T(8,128)}), f32[384,144]{0,1:T(8,128)}) %reduce-scatter.2.cloned.1.call-update) | async-done | bytes 221200 | tf_op jit(solution)/shard_map/reduce_scatter | solution.py:189
  719.5 1.4 copy.136
  720.9 17.5 %all-reduce.11.cloned.1.call-done = f32[384,144]{0,1:T(8,128)} async-done(((f32[384,144]{0,1:T(8,128)}), f32[384,144]{0,1:T(8,128)}) %all-reduce.11.cloned.1.call-update) | async-done | bytes 221200 | tf_op jit(solution)/shard_map/psum | solution.py:190
  (93 shorter events, 17.9 us)
Async XLA Ops:
  7.2 458.3 %copy-start = (bf16[1024,144]{0,1:T(8,128)(2,1)S(1)}, bf16[1024,144]{0,1:T(8,128)(2,1)}, u32[]{:S(2)}) copy-start(bf16[1024,144]{0,1:T(8,128)(2,1)} %param.28) | copy-start | bytes 884740
  7.2 189.5 %all-reduce.5.cloned.1.call-start = ((), (), s32[]{:S(2)}) async-start(), calls=%async_computation.1 | async-start | bytes 9437184 | tf_op jit(solution)/shard_map/psum | solution.py:90
  8.5 0.7 copy-start.7
  13.6 0.7 copy-start.16
  13.6 0.8 copy-start.13
  13.6 447.4 %all-reduce.7.cloned.1.call-start = ((), (), s32[]{:S(2)}) async-start(), calls=%async_computation.2 | async-start | bytes 4194304 | tf_op jit(solution)/shard_map/psum | solution.py:136
  112.8 96.9 %copy-start.12 = (pred[72,128]{1,0:T(8,128)(4,1)}, pred[72,128]{1,0:T(8,128)(4,1)S(1)}, u32[]{:S(2)}) copy-start(pred[72,128]{1,0:T(8,128)(4,1)S(1)} %add_compare_fusion) | copy-start | bytes 27652
  199.5 2.6 copy-start.1
  219.1 81.6 %copy-start.9 = (f32[384,32]{0,1:T(8,128)S(1)}, f32[384,32]{0,1:T(8,128)}, u32[]{:S(2)}) copy-start(f32[384,32]{0,1:T(8,128)} %get-tuple-element.79) | copy-start | bytes 147460
  302.4 11.2 %copy-start.3 = (bf16[384,16,64]{0,2,1:T(8,128)(2,1)}, bf16[384,16,64]{0,2,1:T(8,128)(2,1)S(1)}, u32[]{:S(2)}) copy-start(bf16[384,16,64]{0,2,1:T(8,128)(2,1)S(1)} %maximum_convert_fusion) | copy-start | bytes 2359300
  313.6 6.2 copy-start.10
  318.7 15.7 %copy-start.6 = (f32[4,72,16]{0,2,1:T(8,128)}, f32[4,72,16]{0,2,1:T(8,128)S(1)}, u32[]{:S(2)}) copy-start(f32[4,72,16]{0,2,1:T(8,128)S(1)} %copy.113) | copy-start | bytes 55300
  338.7 145.5 %all-reduce.9.cloned.1.call-start = ((), (), s32[]{:S(2)}) async-start(), calls=%async_computation.3 | async-start | bytes 442368 | tf_op jit(solution)/shard_map/psum | solution.py:162
  340.3 6.9 copy-start.5
  342.2 6.9 copy-start.11
  463.9 2.7 copy-start.8
  464.8 21.2 %copy-start.15 = (s32[4,96,2]{1,2,0:T(2,128)S(1)}, s32[4,96,2]{1,2,0:T(2,128)}, u32[]{:S(2)}) copy-start(s32[4,96,2]{1,2,0:T(2,128)} %param.26) | copy-start | bytes 9220
  466.6 84.4 %all-gather.2.cloned.1.call-start = ((), (), s32[]{:S(2)}) async-start(), calls=%async_computation.4 | async-start | bytes 2506752 | tf_op jit(solution)/shard_map/all_gather | solution.py:166
  486.0 232.9 %reduce-scatter.2.cloned.1.call-start = ((), (), s32[]{:S(2)}) async-start(), calls=%async_computation.5 | async-start | bytes 3760128 | tf_op jit(solution)/shard_map/reduce_scatter | solution.py:189
  550.9 4.3 copy-start.2
  555.2 3.9 copy-start.14
  586.4 132.5 %copy-start.4 = (bf16[384,16,64]{0,2,1:T(8,128)(2,1)S(1)}, bf16[384,16,64]{0,2,1:T(8,128)(2,1)}, u32[]{:S(2)}) copy-start(bf16[384,16,64]{0,2,1:T(8,128)(2,1)} %copy-done.3) | copy-start | bytes 2359300
  586.4 152.0 %all-reduce.11.cloned.1.call-start = ((), (), s32[]{:S(2)}) async-start(), calls=%async_computation.6 | async-start | bytes 442368 | tf_op jit(solution)/shard_map/psum | solution.py:190
Sparse Core Ops, SparseCore 0:
  13.8 182.8 all-reduce.4
  338.8 122.2 all-reduce.6
  466.7 17.4 all-reduce.8
  487.4 63.4 all-gather.1
  586.5 132.2 reduce-scatter.1
  721.0 17.3 all-reduce.10
where the time goes:
time: 757 us; the launch traced here: 747 us
  waiting for transfers between devices  342 us (45%)
  blocking collectives  194 us (26%)
  local copies, waits for them, and re-layouts  102 us (13%)
  matrix products  65.3 us (9%)
  other arithmetic  29.9 us (4%)
  between operations  14.8 us (2%)
    reduce_scatter x1, waiting for transfers between devices, local(): spread = lax.psum_scatter(weighted, 'seq', scatter_dimension=1, tiled=True)  132 us
    psum x1, waiting for transfers between devices, local(): squares, partial_value = lax.psum((squares, partial_value), 'seq')  83.1 us
    pmax x1, blocking collectives, local(): top_score = lax.pmax(req_peak, 'seq')  75.9 us
    psum x1, blocking collectives, local(): lax.psum((weight_sum * rescale, scaled_values), 'seq')  72 us
    all_gather x1, waiting for transfers between devices, local(): shard_rows = lax.all_gather(mid_steps, 'seq', axis=2, tiled=True)  64.8 us
    unnamed x39, local copies, waits for them, and re-layouts  53.7 us
    psum x1, blocking collectives, local(): squares, partial_value = lax.psum((squares, partial_value), 'seq')  45.7 us
    psum x1, waiting for transfers between devices, local(): lax.psum((weight_sum * rescale, scaled_values), 'seq')  26.6 us
  transfers between devices with their start and end apart: 6, of which 6 were waited for; matrix products, arithmetic and copies ran while one was open for 11% of the time, Pallas kernels for 0%

commit v1 on v0

--- a/solution.py
+++ b/solution.py
@@ -159,7 +159,8 @@
     attended = (
         (numerator / denominator[..., None]).reshape(row_count, cols_loc).astype(jnp.bfloat16)
     )
-    projected = lax.psum(jnp.dot(attended, w_out, preferred_element_type=jnp.float32), "col")
+    body = jnp.dot(attended, w_out, preferred_element_type=jnp.float32)
+    projected = jax.lax.all_gather(body, "col").sum(axis=0)
     residual = (wide_in.reshape(row_count, width_loc) + projected).astype(jnp.bfloat16)
     chosen = route_ids.reshape(row_count, 2)
     mid_steps = residual.reshape(step_count, requests, width_loc)

time: 757 us -> 735 us (0.971)
  waiting for transfers between devices: 342 us -> 321 us
    unnamed x6, waiting for transfers between devices: 0.1 us -> 133 us
    reduce_scatter x1 -> x0, waiting for transfers between devices: 132 us -> none  [local(): spread = lax.psum_scatter(weighted, 'seq', scatter_dimension=1, tiled=True)]
    psum x1 -> x0, waiting for transfers between devices: 17.3 us -> none  [local(): lax.psum(jnp.dot(attended, w_out, preferred_element_type=jnp.float32), 'c...]
    unnamed x39 -> x40, local copies, waits for them, and re-layouts: 53.7 us -> 58.8 us
  transfers between devices with their start and end apart: 6 -> 5, of which waited for: 6 -> 5; matrix products, arithmetic and copies ran while one was open for 11% -> 11% of each run, Pallas kernels for 0% -> 0%
where the time goes in v1:
time: 735 us; the launch traced here: 725 us
  waiting for transfers between devices  321 us (44%)
  blocking collectives  196 us (27%)
  local copies, waits for them, and re-layouts  99.9 us (14%)
  matrix products  64.6 us (9%)
  other arithmetic  28.4 us (4%)
  between operations  14.5 us (2%)
    unnamed x6, waiting for transfers between devices  133 us
    psum x1, waiting for transfers between devices, local(): squares, partial_value = lax.psum((squares, partial_value), 'seq')  83.1 us
    pmax x1, blocking collectives, local(): top_score = lax.pmax(req_peak, 'seq')  75.9 us
    psum x1, blocking collectives, local(): lax.psum((weight_sum * rescale, scaled_values), 'seq')  72 us
    all_gather x1, waiting for transfers between devices, local(): shard_rows = lax.all_gather(mid_steps, 'seq', axis=2, tiled=True)  61.5 us
    unnamed x40, local copies, waits for them, and re-layouts  58.8 us
    psum x1, blocking collectives, local(): squares, partial_value = lax.psum((squares, partial_value), 'seq')  45.7 us
    psum x1, waiting for transfers between devices, local(): lax.psum((weight_sum * rescale, scaled_values), 'seq')  26.5 us
  transfers between devices with their start and end apart: 5, of which 5 were waited for; matrix products, arithmetic and copies ran while one was open for 11% of the time, Pallas kernels for 0%

profile of v1, /device:TPU:0, one launch (start us, length us, event | category | flops | bytes accessed | tf_op | source)
XLA Modules:
  0.0 724.8 jit_solution(3737002149559758724)
XLA Ops:
  7.2 1.2 fusion.26
  9.4 1.2 copy.182
  10.6 3.0 fusion.36
  14.5 1.7 fusion.2
  16.3 45.7 %psum.36 = f32[4,96]{1,0:T(4,128)S(1)} all-reduce(f32[4,96]{1,0:T(4,128)S(1)} %get-tuple-element.66), channel_id=1, replica_groups=mesh['seq'=16,'col'=2] {'seq'}, use_global_device_ids=true, to_apply=%region_5.6 | all-reduce | flops 384 | bytes 3072 | tf_op jit(solution)/shard_map/psum | solution.py:90
  62.1 24.6 %copy.141 = bf16[72,128,1024]{1,2,0:T(8,128)(2,1)} copy(bf16[72,128,1024]{2,1,0:T(8,128)(2,1)} %param.21) | data formatting | bytes 37748736 | tf_op args[1]
  86.7 24.7 %copy.146 = bf16[72,128,1024]{1,2,0:T(8,128)(2,1)} copy(bf16[72,128,1024]{2,1,0:T(8,128)(2,1)} %param.22) | data formatting | bytes 37748736 | tf_op args[2]
  111.5 1.1 select_reduce_fusion
  113.7 83.1 %all-reduce.4.cloned.1.call-done = f32[384,3072]{1,0:T(8,128)} async-done(((f32[384,3072]{1,0:T(8,128)}), f32[384,3072]{1,0:T(8,128)}) %all-reduce.4.cloned.1.call-update) | async-done | bytes 4718608 | tf_op jit(solution)/shard_map/psum | solution.py:90
  196.7 2.8 broadcast_multiply_fusion
  199.5 1.6 fusion.35
  204.8 2.6 copy.151
  207.4 2.2 copy.142
  209.7 9.4 %bitcast_reduce_fusion = (f32[4,72,16]{0,2,1:T(8,128)S(1)}, f32[72,16,4,128]{3,2,1,0:T(4,128)S(1)}) fusion(pred[72,128]{1,0:T(8,128)(4,1)S(1)} %add_compare_fusion, bf16[4,72,16,64]{3,0,2,1:T(4,128)(2,1)} %copy.142, bf16[72,128,16,64]{1,3,2,0:T(8,128)(2,1)} %bitcast.109), kind=kOutput, calls=%fused_computation.8 | convolution fusion | flops 77262336 | bytes 21851136 | tf_op jit(solution)/shard_map/pthd,nphd->npth/dot_general | solution.py:110
  220.4 75.9 %pmax.7 = f32[4,96,16]{1,2,0:T(8,128)} all-reduce(f32[4,96,16]{1,2,0:T(8,128)S(1)} %select_reduce_fusion.2), channel_id=1, replica_groups=mesh['seq'=16,'col'=2] {'seq'}, use_global_device_ids=true, to_apply=%region_9.10 | all-reduce | flops 6144 | bytes 49152 | tf_op jit(solution)/shard_map/pmax | solution.py:131
  296.3 1.4 select_reduce_fusion.1
  297.7 3.0 copy.149
  300.7 1.6 multiply_subtract_fusion
  302.4 1.6 convert_element_type.90
  304.0 4.3 copy.150
  308.3 5.3 fusion.37
  313.6 3.7 copy.152
  317.3 1.4 copy.145
  318.7 1.1 fusion.23
  320.5 14.0 %convolution_bitcast_fusion = f32[4,72,16,64]{3,0,2,1:T(4,128)S(1)} fusion(bf16[72,128,16,64]{1,3,2,0:T(8,128)(2,1)} %bitcast.110, f32[72,16,4,128]{3,2,1,0:T(4,128)S(1)} %get-tuple-element.81, f32[4,72,16]{0,2,1:T(8,128)S(1)} %copy.145, pred[72,128]{1,0:T(8,128)(4,1)} %copy-done.12), kind=kOutput, calls=%fused_computation.24 | convolution fusion | flops 78446592 | bytes 22440960 | tf_op jit(solution)/shard_map/npth,pthd->nphd/dot_general | solution.py:121
  334.5 4.2 bitcast_multiply_fusion.1
  338.8 1.6 slice.111
  340.3 1.9 reshape.361
  342.3 5.0 fusion.20
  347.2 1.9 copy.159
  349.2 1.6 fusion.24
  350.8 3.2 copy.157
  354.0 3.7 fusion.12
  357.6 3.1 copy.158
  361.7 72.0 %psum.38 = f32[4,96,16]{1,2,0:T(8,128)S(1)} all-reduce(f32[4,96,16]{1,2,0:T(8,128)S(1)} %fusion.16), channel_id=1, replica_groups=mesh['seq'=16,'col'=2] {'seq'}, use_global_device_ids=true, to_apply=%region_13.14 | all-reduce | flops 6144 | bytes 49152 | tf_op jit(solution)/shard_map/psum | solution.py:136
  434.5 26.5 %all-reduce.6.cloned.1.call-done = f32[4,96,16,64]{1,3,2,0:T(8,128)} async-done(((f32[4,96,16,64]{1,3,2,0:T(8,128)}), f32[4,96,16,64]{1,3,2,0:T(8,128)}) %all-reduce.6.cloned.1.call-update) | async-done | bytes 1572880 | tf_op jit(solution)/shard_map/psum | solution.py:136
  461.1 2.8 fusion.9
  465.8 2.1 all-gather
  470.1 61.5 %all-gather.3.cloned.1.call-done = bf16[4,96,2304]{1,2,0:T(8,128)(2,1)} async-done(((bf16[4,96,144]{1,2,0:T(8,128)(2,1)}), bf16[4,96,2304]{1,2,0:T(8,128)(2,1)}) %all-gather.3.cloned.1.call-update) | async-done | bytes 1769488 | tf_op jit(solution)/shard_map/all_gather | solution.py:167
  531.5 2.4 multiply_reduce_fusion
  534.1 2.4 copy.165
  536.5 2.1 select_reduce_fusion.4
  538.6 10.3 %broadcast_multiply_fusion.1 = f32[384,4,720]{0,2,1:T(8,128)S(1)} fusion(f32[384]{0:T(512)S(1)} %rsqrt.27, bf16[384,2304,1]{1,0,2:T(8,128)(2,1)} %bitcast.113, bf16[4,2304,720]{1,2,0:T(8,128)(2,1)} %bitcast.123), kind=kOutput, calls=%fused_computation.19 | convolution fusion | flops 5097185280 | bytes 19465728 | tf_op jit(solution)/shard_map/rc,ecf->ref/dot_general | solution.py:169
  548.9 9.8 %fusion = f32[384,2304]{1,0:T(8,128)} fusion(bf16[4,360,2304]{2,1,0:T(8,128)(2,1)} %param.31, f32[384,4]{0,1:T(4,128)S(1)} %select_add_fusion, f32[384,4,720]{0,2,1:T(8,128)S(1)} %broadcast_multiply_fusion.1), kind=kOutput, calls=%fused_computation.1 | convolution fusion | flops 2557550592 | bytes 14604288 | tf_op jit(solution)/shard_map/ref,efd->red/dot_general | solution.py:188
  558.7 5.2 copy.178
  563.9 132.8 %reduce-scatter.4.cloned.1.call-done = f32[144,384]{1,0:T(8,128)} async-done(((f32[2304,384]{1,0:T(8,128)}), f32[144,384]{1,0:T(8,128)}) %reduce-scatter.4.cloned.1.call-update) | async-done | bytes 221200
  697.6 1.4 copy.169
  698.9 17.3 %all-reduce.8.cloned.1.call-done = f32[384,144]{0,1:T(8,128)} async-done(((f32[384,144]{0,1:T(8,128)}), f32[384,144]{0,1:T(8,128)}) %all-reduce.8.cloned.1.call-update) | async-done | bytes 221200 | tf_op jit(solution)/shard_map/psum | solution.py:191
  (93 shorter events, 17.2 us)
Async XLA Ops:
  7.2 458.3 %copy-start = (bf16[1024,144]{0,1:T(8,128)(2,1)S(1)}, bf16[1024,144]{0,1:T(8,128)(2,1)}, u32[]{:S(2)}) copy-start(bf16[1024,144]{0,1:T(8,128)(2,1)} %param.28) | copy-start | bytes 884740
  7.2 189.5 %all-reduce.4.cloned.1.call-start = ((), (), s32[]{:S(2)}) async-start(), calls=%async_computation.1 | async-start | bytes 9437184 | tf_op jit(solution)/shard_map/psum | solution.py:90
  8.5 0.7 copy-start.6
  13.6 0.7 copy-start.16
  13.6 0.8 copy-start.13
  13.6 447.4 %all-reduce.6.cloned.1.call-start = ((), (), s32[]{:S(2)}) async-start(), calls=%async_computation.2 | async-start | bytes 4194304 | tf_op jit(solution)/shard_map/psum | solution.py:136
  112.8 96.9 %copy-start.12 = (pred[72,128]{1,0:T(8,128)(4,1)}, pred[72,128]{1,0:T(8,128)(4,1)S(1)}, u32[]{:S(2)}) copy-start(pred[72,128]{1,0:T(8,128)(4,1)S(1)} %add_compare_fusion) | copy-start | bytes 27652
  199.5 2.6 copy-start.1
  219.1 81.6 %copy-start.9 = (f32[384,32]{0,1:T(8,128)S(1)}, f32[384,32]{0,1:T(8,128)}, u32[]{:S(2)}) copy-start(f32[384,32]{0,1:T(8,128)} %get-tuple-element.79) | copy-start | bytes 147460
  302.4 11.2 %copy-start.3 = (bf16[384,16,64]{0,2,1:T(8,128)(2,1)}, bf16[384,16,64]{0,2,1:T(8,128)(2,1)S(1)}, u32[]{:S(2)}) copy-start(bf16[384,16,64]{0,2,1:T(8,128)(2,1)S(1)} %maximum_convert_fusion) | copy-start | bytes 2359300
  313.6 6.2 copy-start.10
  318.7 15.7 %copy-start.8 = (f32[4,72,16]{0,2,1:T(8,128)}, f32[4,72,16]{0,2,1:T(8,128)S(1)}, u32[]{:S(2)}) copy-start(f32[4,72,16]{0,2,1:T(8,128)S(1)} %copy.145) | copy-start | bytes 55300
  338.7 192.8 %all-gather.3.cloned.1.call-start = ((), (), s32[]{:S(2)}) async-start(), calls=%async_computation.3 | async-start | bytes 2506752 | tf_op jit(solution)/shard_map/all_gather | solution.py:167
  340.3 6.9 copy-start.5
  342.3 6.9 copy-start.11
  465.5 3.5 copy-start.7
  465.5 4.4 copy-start.15
  469.7 227.0 %reduce-scatter.4.cloned.1.call-start = ((), (), s32[]{:S(2)}) async-start(), calls=%async_computation.5 | async-start | bytes 3760128
  531.5 2.5 copy-start.2
  534.0 2.5 copy-start.14
  563.8 133.1 %copy-start.4 = (bf16[384,16,64]{0,2,1:T(8,128)(2,1)S(1)}, bf16[384,16,64]{0,2,1:T(8,128)(2,1)}, u32[]{:S(2)}) copy-start(bf16[384,16,64]{0,2,1:T(8,128)(2,1)} %copy-done.3) | copy-start | bytes 2359300
  563.8 152.4 %all-reduce.8.cloned.1.call-start = ((), (), s32[]{:S(2)}) async-start(), calls=%async_computation.4 | async-start | bytes 442368 | tf_op jit(solution)/shard_map/psum | solution.py:191
Sparse Core Ops, SparseCore 0:
  13.8 182.9 all-reduce.3
  338.8 122.1 all-reduce.5
  469.8 61.7 all-gather.2
  564.0 132.6 reduce-scatter.3
  698.9 17.3 all-reduce.7
